TPU v7x, 32 devices: a whole 2x2x4 slice. The times are simulated.
32 devices in a mesh: row: 8 (over z, core), col: 2 (over x), rep: 2 (over y).
Axes of the slice: x: 2, y: 2, z: 4, core: 2. Of those that a mesh axis runs over, the one named last changes fastest.
Arguments:
- features: bfloat16 [16384, 512], P(('rep', 'col', 'row')), parts along dimension 0, may hold values from -6 to 6
- weights: bfloat16 [512, 512], replicated, may hold values from -0.25 to 0.25
- bias_vector: float32 [512], replicated, may hold values from -3 to 3
- tile_values: bfloat16 [16, 2, 128, 128, 128], P(('rep', 'row'), 'col'), parts along dimension 0, may hold values from -0.15625 to 0.15625
- tile_rows: int32 [16, 2, 128], P(('rep', 'row'), 'col'), parts along dimension 0, may hold values from 0 to 7, as said below
- tile_cols: int32 [16, 2, 128], P(('rep', 'row'), 'col'), parts along dimension 0, may hold values from 0 to 31, as said below
- tile_counts: int32 [16, 2], P(('rep', 'row'), 'col'), parts along dimension 0, may hold values from 8 to 128, as said below
- cotangent: bfloat16 [16384, 512], P(('rep', 'row', 'col')), parts along dimension 0, may hold values from -6 to 6
Outputs:
- activated: bfloat16 [16384, 512], P(('rep', 'row', 'col')), parts along dimension 0
- weight_grad: float32 [1024, 512], P('rep'), parts along dimension 0
- bias_grad: float32 [1024], P('rep'), parts along dimension 0
- feature_grad: bfloat16 [16384, 512], P(('rep', 'col', 'row')), parts along dimension 0
There are 2 independent parts, one for each index of `rep`. A program takes and returns all parts, laid end to end along the dimension named above; an argument that names none is the same for every part. Nothing has to cross between parts.
Inputs may be any that keep to these rules, and one draw needn't show every extreme that they name: `tile_counts`: live slots of every grid cell; some cell holds exactly 128. `tile_cols`: among a cell's first tile_counts slots the column indices never fall; later slots hold arbitrary indices of the range. A (row, column) pair may repeat, and then its tiles add. `tile_rows`: slots past a cell's count hold arbitrary indices of the range.
All inputs are finite; a program needn't handle non-finite values.
Results may differ from a plain program's by a relative error of at most 0.01.
Values may be sent and summed in bfloat16 or wider, within the bound.
A program may use at most 128 MiB of HBM per device.

v0:
```python
import math

import jax
import jax.numpy as jnp
from jax import lax
from jax.sharding import PartitionSpec as P

slot_group = 16


def tile_range(cols_in, live_count, first_block, last_block):
    slots = jnp.arange(cols_in.shape[0], dtype=jnp.int32)
    live = slots < live_count
    lower = jnp.sum((live & (cols_in < first_block)).astype(jnp.int32))
    upper = jnp.sum((live & (cols_in < last_block)).astype(jnp.int32))
    return (lower, upper)


def group_slots(tiles, rows_in, cols_in, begin, upper):
    limit = tiles.shape[0] - slot_group
    start = jnp.minimum(begin, limit)
    tile_group = lax.dynamic_slice_in_dim(tiles, start, slot_group, 0)
    row_group = lax.dynamic_slice_in_dim(rows_in, start, slot_group, 0)
    col_group = lax.dynamic_slice_in_dim(cols_in, start, slot_group, 0)
    slots = start + jnp.arange(slot_group, dtype=jnp.int32)
    live = ((slots >= begin) & (slots < upper)).astype(jnp.float32)
    return (tile_group, row_group, col_group, live)


def forward_tiles(carry, tiles, rows_in, cols_in, piece, first_block, lower, upper):
    edge = tiles.shape[-1]
    blocks = piece.reshape(-1, edge, piece.shape[-1])
    block_count = blocks.shape[0]
    group_total = (upper - lower + slot_group - 1) // slot_group

    def forward_step(group_index, accum):
        begin = lower + group_index * slot_group
        tile_group, row_group, col_group, live = group_slots(tiles, rows_in, cols_in, begin, upper)
        local = jnp.clip(col_group - first_block, 0, block_count - 1)
        taken = jnp.take(blocks, local, axis=0)
        product = jnp.einsum("gij,gjf->gif", tile_group, taken, preferred_element_type=jnp.float32)
        return accum.at[row_group].add(product * live[:, None, None])

    return lax.fori_loop(0, group_total, forward_step, carry)


def backward_tiles(carry, tiles, rows_in, cols_in, grad_blocks, first_block, lower, upper):
    block_count = carry.shape[0]
    group_total = (upper - lower + slot_group - 1) // slot_group

    def backward_step(group_index, accum):
        begin = lower + group_index * slot_group
        tile_group, row_group, col_group, live = group_slots(tiles, rows_in, cols_in, begin, upper)
        taken = jnp.take(grad_blocks, row_group, axis=0)
        product = jnp.einsum("gji,gjf->gif", tile_group, taken, preferred_element_type=jnp.float32)
        local = jnp.clip(col_group - first_block, 0, block_count - 1)
        return accum.at[local].add(product * live[:, None, None])

    return lax.fori_loop(0, group_total, backward_step, carry)


def on_device(
    features, weights, bias_vector, tile_values, tile_rows, tile_cols, tile_counts, cotangent
):
    tiles = tile_values[0, 0]
    rows_in = tile_rows[0, 0]
    cols_in = tile_cols[0, 0]
    live_count = tile_counts[0, 0]
    row_devs = lax.axis_size("row")
    col_devs = lax.axis_size("col")
    local_rows = features.shape[0]
    width = features.shape[1]
    edge = tiles.shape[-1]
    row_tiles = local_rows * col_devs // edge
    col_tiles = local_rows * row_devs // edge
    empty_rows = jnp.zeros((row_tiles, edge, width), jnp.float32)
    column_block = lax.all_gather(features, "row", axis=0, tiled=True)
    lower, upper = tile_range(cols_in, live_count, 0, col_tiles)
    partial_value = forward_tiles(
        empty_rows, tiles, rows_in, cols_in, column_block, 0, lower, upper
    )
    gathered = lax.psum_scatter(
        partial_value.reshape(row_tiles * edge, width).astype(jnp.bfloat16),
        "col",
        scatter_dimension=0,
        tiled=True,
    )
    pre = jnp.dot(gathered, weights, preferred_element_type=jnp.float32) + bias_vector
    sig = jax.nn.sigmoid(pre)
    activated = (pre * sig).astype(jnp.bfloat16)
    dpre = (cotangent.astype(jnp.float32) * sig * (1.0 + pre * (1.0 - sig))).astype(jnp.bfloat16)
    weight_local = lax.dot_general(
        gathered, dpre, (((0,), (0,)), ((), ())), preferred_element_type=jnp.float32
    )
    bias_local = jnp.sum(dpre.astype(jnp.float32), axis=0)
    weight_total, bias_total = lax.psum((weight_local, bias_local), ("row", "col"))
    scale = 1.0 / math.sqrt(local_rows * row_devs * col_devs)
    weight_grad = weight_total * scale
    bias_grad = bias_total * scale
    dgathered = lax.dot_general(
        dpre, weights, (((1,), (1,)), ((), ())), preferred_element_type=jnp.float32
    ).astype(jnp.bfloat16)
    row_block = lax.all_gather(dgathered, "col", axis=0, tiled=True)
    grad_blocks = row_block.reshape(row_tiles, edge, width)
    lower, upper = tile_range(cols_in, live_count, 0, col_tiles)
    empty_cols = jnp.zeros((col_tiles, edge, width), jnp.float32)
    term = backward_tiles(empty_cols, tiles, rows_in, cols_in, grad_blocks, 0, lower, upper)
    feature_sum = lax.psum_scatter(
        term.reshape(col_tiles * edge, width).astype(jnp.bfloat16),
        "row",
        scatter_dimension=0,
        tiled=True,
    )
    return (activated, weight_grad, bias_grad, feature_sum)


def solution(mesh):
    in_specs = (
        P(("rep", "col", "row"), None),
        P(),
        P(),
        P(("rep", "row"), "col", None, None, None),
        P(("rep", "row"), "col", None),
        P(("rep", "row"), "col", None),
        P(("rep", "row"), "col"),
        P(("rep", "row", "col"), None),
    )
    out_specs = (
        P(("rep", "row", "col"), None),
        P("rep", None),
        P("rep"),
        P(("rep", "col", "row"), None),
    )
    return jax.shard_map(
        on_device, mesh=mesh, in_specs=in_specs, out_specs=out_specs, check_vma=False
    )
```

profile of v0, /device:TPU:4, one launch (start us, length us, event | category | flops | bytes accessed | tf_op | source)
XLA Modules:
  0.0 438.8 jit_solution(4892693256379624457)
XLA Ops:
  8.6 1.3 fusion.13
  11.1 46.9 %all-gather.3.cloned.1.call-done = bf16[4096,512]{1,0:T(8,128)(2,1)} async-done(((bf16[512,512]{1,0:T(8,128)(2,1)}), bf16[4096,512]{1,0:T(8,128)(2,1)}) %all-gather.3.cloned.1.call-update) | async-done | bytes 4194320 | tf_op jit(solution)/shard_map/all_gather | solution.py:77
  58.3 105.6 %while.20 = (s32[]{:T(128)}, f32[8,128,512]{2,1,0:T(8,128)S(1)}, s32[]{:T(128)}, s32[]{:T(128)}, s32[128]{0:T(128)}, /*index=5*/bf16[128,128,128]{2,1,0:T(8,128)...) while((s32[]{:T(128)}, f32[8,128,512]{2,1,0:T(8,128)S(1)}, ...), condition=%wide.region_4.5_spmd, body=%wide.region_2.4_spmd.sunk | while | flops 271582464 | bytes 23597892 | solution.py:44
  58.9 0.7 compare_select_fusion.8
  59.6 1.3 compare_and_fusion.4
  60.9 4.3 gather_fusion
  65.2 4.5 %convolution_multiply_fusion.4 = f32[16,128,512]{2,1,0:T(8,128)} fusion(f32[16]{0:T(128)S(1)} %get-tuple-element.267, bf16[16,128,512]{2,1,0:T(8,128)(2,1)} %gather_fusion, pred[16]{0:T(512)(128)(4,1)S(1)} %get-tuple-element.269, bf16[128,128,128]{2,1,0:T(8,128)(2,1)} %get-tuple-element.315, s32[]{:T(128)S(6)} %select_n.58), kind=kOutput, calls=%fused_computation.4.clone.1 | convolution fusion | flops 270532608 | bytes 6815828 | tf_op jit(solution)/shard_map/while/body/gij,gjf->gif/dot_general | solution.py:41
  69.7 6.2 %scatter_fusion = f32[8,128,512]{2,1,0:T(8,128)S(1)} fusion(f32[8,128,512]{2,1,0:T(8,128)S(1)} %get-tuple-element.297, s32[16]{0:T(128)S(1)} %compare_select_fusion.8, f32[16,128,512]{2,1,0:T(8,128)} %convolution_multiply_fusion.4), kind=kCustom, calls=%fused_computation.2.clone.1 | custom fusion | flops 1048576 | bytes 12582976 | tf_op jit(solution)/shard_map/while/body/scatter-add | solution.py:42
  76.5 0.7 compare_select_fusion.8
  77.2 1.3 compare_and_fusion.4
  78.5 4.3 gather_fusion
  82.8 4.5 %convolution_multiply_fusion.4 = f32[16,128,512]{2,1,0:T(8,128)} fusion(f32[16]{0:T(128)S(1)} %get-tuple-element.267, bf16[16,128,512]{2,1,0:T(8,128)(2,1)} %gather_fusion, pred[16]{0:T(512)(128)(4,1)S(1)} %get-tuple-element.269, bf16[128,128,128]{2,1,0:T(8,128)(2,1)} %get-tuple-element.315, s32[]{:T(128)S(6)} %select_n.58), kind=kOutput, calls=%fused_computation.4.clone.1 | convolution fusion | flops 270532608 | bytes 6815828 | tf_op jit(solution)/shard_map/while/body/gij,gjf->gif/dot_general | solution.py:41
  87.3 6.1 %scatter_fusion = f32[8,128,512]{2,1,0:T(8,128)S(1)} fusion(f32[8,128,512]{2,1,0:T(8,128)S(1)} %get-tuple-element.297, s32[16]{0:T(128)S(1)} %compare_select_fusion.8, f32[16,128,512]{2,1,0:T(8,128)} %convolution_multiply_fusion.4), kind=kCustom, calls=%fused_computation.2.clone.1 | custom fusion | flops 1048576 | bytes 12582976 | tf_op jit(solution)/shard_map/while/body/scatter-add | solution.py:42
  94.1 0.7 compare_select_fusion.8
  94.8 1.3 compare_and_fusion.4
  96.1 4.3 gather_fusion
  100.4 4.5 %convolution_multiply_fusion.4 = f32[16,128,512]{2,1,0:T(8,128)} fusion(f32[16]{0:T(128)S(1)} %get-tuple-element.267, bf16[16,128,512]{2,1,0:T(8,128)(2,1)} %gather_fusion, pred[16]{0:T(512)(128)(4,1)S(1)} %get-tuple-element.269, bf16[128,128,128]{2,1,0:T(8,128)(2,1)} %get-tuple-element.315, s32[]{:T(128)S(6)} %select_n.58), kind=kOutput, calls=%fused_computation.4.clone.1 | convolution fusion | flops 270532608 | bytes 6815828 | tf_op jit(solution)/shard_map/while/body/gij,gjf->gif/dot_general | solution.py:41
  104.9 6.2 %scatter_fusion = f32[8,128,512]{2,1,0:T(8,128)S(1)} fusion(f32[8,128,512]{2,1,0:T(8,128)S(1)} %get-tuple-element.297, s32[16]{0:T(128)S(1)} %compare_select_fusion.8, f32[16,128,512]{2,1,0:T(8,128)} %convolution_multiply_fusion.4), kind=kCustom, calls=%fused_computation.2.clone.1 | custom fusion | flops 1048576 | bytes 12582976 | tf_op jit(solution)/shard_map/while/body/scatter-add | solution.py:42
  111.7 0.7 compare_select_fusion.8
  112.4 1.3 compare_and_fusion.4
  113.7 4.3 gather_fusion
  118.0 4.5 %convolution_multiply_fusion.4 = f32[16,128,512]{2,1,0:T(8,128)} fusion(f32[16]{0:T(128)S(1)} %get-tuple-element.267, bf16[16,128,512]{2,1,0:T(8,128)(2,1)} %gather_fusion, pred[16]{0:T(512)(128)(4,1)S(1)} %get-tuple-element.269, bf16[128,128,128]{2,1,0:T(8,128)(2,1)} %get-tuple-element.315, s32[]{:T(128)S(6)} %select_n.58), kind=kOutput, calls=%fused_computation.4.clone.1 | convolution fusion | flops 270532608 | bytes 6815828 | tf_op jit(solution)/shard_map/while/body/gij,gjf->gif/dot_general | solution.py:41
  122.5 6.2 %scatter_fusion = f32[8,128,512]{2,1,0:T(8,128)S(1)} fusion(f32[8,128,512]{2,1,0:T(8,128)S(1)} %get-tuple-element.297, s32[16]{0:T(128)S(1)} %compare_select_fusion.8, f32[16,128,512]{2,1,0:T(8,128)} %convolution_multiply_fusion.4), kind=kCustom, calls=%fused_computation.2.clone.1 | custom fusion | flops 1048576 | bytes 12582976 | tf_op jit(solution)/shard_map/while/body/scatter-add | solution.py:42
  129.3 0.7 compare_select_fusion.8
  130.0 1.3 compare_and_fusion.4
  131.3 4.3 gather_fusion
  135.6 4.5 %convolution_multiply_fusion.4 = f32[16,128,512]{2,1,0:T(8,128)} fusion(f32[16]{0:T(128)S(1)} %get-tuple-element.267, bf16[16,128,512]{2,1,0:T(8,128)(2,1)} %gather_fusion, pred[16]{0:T(512)(128)(4,1)S(1)} %get-tuple-element.269, bf16[128,128,128]{2,1,0:T(8,128)(2,1)} %get-tuple-element.315, s32[]{:T(128)S(6)} %select_n.58), kind=kOutput, calls=%fused_computation.4.clone.1 | convolution fusion | flops 270532608 | bytes 6815828 | tf_op jit(solution)/shard_map/while/body/gij,gjf->gif/dot_general | solution.py:41
  140.1 6.1 %scatter_fusion = f32[8,128,512]{2,1,0:T(8,128)S(1)} fusion(f32[8,128,512]{2,1,0:T(8,128)S(1)} %get-tuple-element.297, s32[16]{0:T(128)S(1)} %compare_select_fusion.8, f32[16,128,512]{2,1,0:T(8,128)} %convolution_multiply_fusion.4), kind=kCustom, calls=%fused_computation.2.clone.1 | custom fusion | flops 1048576 | bytes 12582976 | tf_op jit(solution)/shard_map/while/body/scatter-add | solution.py:42
  146.9 0.7 compare_select_fusion.8
  147.6 1.3 compare_and_fusion.4
  148.9 4.3 gather_fusion
  153.1 4.5 %convolution_multiply_fusion.4 = f32[16,128,512]{2,1,0:T(8,128)} fusion(f32[16]{0:T(128)S(1)} %get-tuple-element.267, bf16[16,128,512]{2,1,0:T(8,128)(2,1)} %gather_fusion, pred[16]{0:T(512)(128)(4,1)S(1)} %get-tuple-element.269, bf16[128,128,128]{2,1,0:T(8,128)(2,1)} %get-tuple-element.315, s32[]{:T(128)S(6)} %select_n.58), kind=kOutput, calls=%fused_computation.4.clone.1 | convolution fusion | flops 270532608 | bytes 6815828 | tf_op jit(solution)/shard_map/while/body/gij,gjf->gif/dot_general | solution.py:41
  157.6 6.2 %scatter_fusion = f32[8,128,512]{2,1,0:T(8,128)S(1)} fusion(f32[8,128,512]{2,1,0:T(8,128)S(1)} %get-tuple-element.297, s32[16]{0:T(128)S(1)} %compare_select_fusion.8, f32[16,128,512]{2,1,0:T(8,128)} %convolution_multiply_fusion.4), kind=kCustom, calls=%fused_computation.2.clone.1 | custom fusion | flops 1048576 | bytes 12582976 | tf_op jit(solution)/shard_map/while/body/scatter-add | solution.py:42
  163.9 1.1 convert_element_type.51
  165.0 53.7 %reduce-scatter.3.cloned.1.call-done = bf16[512,512]{1,0:T(8,128)(2,1)} async-done(((bf16[1024,512]{1,0:T(8,128)(2,1)}), bf16[512,512]{1,0:T(8,128)(2,1)}) %reduce-scatter.3.cloned.1.call-update) | async-done | bytes 524304 | tf_op jit(solution)/shard_map/reduce_scatter | solution.py:82
  218.7 2.7 convert_reduce_fusion
  221.4 1.3 convolution_convert_fusion
  222.8 6.4 %copy.12 = bf16[1,1,128,128,128]{3,4,2,1,0:T(8,128)(2,1)} copy(bf16[1,1,128,128,128]{4,3,2,1,0:T(8,128)(2,1)} %bitcast.22) | data formatting | bytes 8388608 | tf_op args[3]
  229.2 1.4 fusion.14
  230.7 13.5 %all-gather.5.cloned.1.call-done = bf16[1024,512]{1,0:T(8,128)(2,1)} async-done(((bf16[512,512]{1,0:T(8,128)(2,1)}), bf16[1024,512]{1,0:T(8,128)(2,1)}) %all-gather.5.cloned.1.call-update) | async-done | bytes 1048592 | tf_op jit(solution)/shard_map/all_gather | solution.py:103
  244.2 4.3 broadcast_in_dim.40
  248.5 96.5 %while.21 = (s32[]{:T(128)}, f32[32,128,512]{2,1,0:T(8,128)}, s32[]{:T(128)}, s32[]{:T(128)}, s32[128]{0:T(128)S(1)}, /*index=5*/bf16[128,128,128]{1,2,0:T(8,128...) while((s32[]{:T(128)}, f32[32,128,512]{2,1,0:T(8,128)}, ...), condition=%wide.region_11.12_spmd, body=%wide.region_9.11_spmd.sunk | while | flops 271582464 | bytes 23597892 | solution.py:59
  249.9 1.9 gather_fusion.1
  251.8 3.8 convolution_multiply_fusion.5
  255.5 9.0 %scatter_fusion.1 = f32[32,128,512]{2,1,0:T(8,128)} fusion(f32[32,128,512]{2,1,0:T(8,128)} %get-tuple-element.339, s32[16]{0:T(128)S(1)} %compare_select_fusion.9, f32[16,128,512]{2,1,0:T(8,128)} %convolution_multiply_fusion.5), kind=kCustom, calls=%fused_computation.3.clone.1 | custom fusion | flops 1048576 | bytes 12582976 | tf_op jit(solution)/shard_map/while/body/scatter-add | solution.py:57
  265.8 1.9 gather_fusion.1
  267.8 3.8 convolution_multiply_fusion.5
  271.5 9.1 %scatter_fusion.1 = f32[32,128,512]{2,1,0:T(8,128)} fusion(f32[32,128,512]{2,1,0:T(8,128)} %get-tuple-element.339, s32[16]{0:T(128)S(1)} %compare_select_fusion.9, f32[16,128,512]{2,1,0:T(8,128)} %convolution_multiply_fusion.5), kind=kCustom, calls=%fused_computation.3.clone.1 | custom fusion | flops 1048576 | bytes 12582976 | tf_op jit(solution)/shard_map/while/body/scatter-add | solution.py:57
  282.0 1.9 gather_fusion.1
  283.9 3.8 convolution_multiply_fusion.5
  287.6 9.1 %scatter_fusion.1 = f32[32,128,512]{2,1,0:T(8,128)} fusion(f32[32,128,512]{2,1,0:T(8,128)} %get-tuple-element.339, s32[16]{0:T(128)S(1)} %compare_select_fusion.9, f32[16,128,512]{2,1,0:T(8,128)} %convolution_multiply_fusion.5), kind=kCustom, calls=%fused_computation.3.clone.1 | custom fusion | flops 1048576 | bytes 12582976 | tf_op jit(solution)/shard_map/while/body/scatter-add | solution.py:57
  298.0 1.9 gather_fusion.1
  300.0 3.8 convolution_multiply_fusion.5
  303.7 8.8 %scatter_fusion.1 = f32[32,128,512]{2,1,0:T(8,128)} fusion(f32[32,128,512]{2,1,0:T(8,128)} %get-tuple-element.339, s32[16]{0:T(128)S(1)} %compare_select_fusion.9, f32[16,128,512]{2,1,0:T(8,128)} %convolution_multiply_fusion.5), kind=kCustom, calls=%fused_computation.3.clone.1 | custom fusion | flops 1048576 | bytes 12582976 | tf_op jit(solution)/shard_map/while/body/scatter-add | solution.py:57
  313.9 1.9 gather_fusion.1
  315.8 3.8 convolution_multiply_fusion.5
  319.6 9.2 %scatter_fusion.1 = f32[32,128,512]{2,1,0:T(8,128)} fusion(f32[32,128,512]{2,1,0:T(8,128)} %get-tuple-element.339, s32[16]{0:T(128)S(1)} %compare_select_fusion.9, f32[16,128,512]{2,1,0:T(8,128)} %convolution_multiply_fusion.5), kind=kCustom, calls=%fused_computation.3.clone.1 | custom fusion | flops 1048576 | bytes 12582976 | tf_op jit(solution)/shard_map/while/body/scatter-add | solution.py:57
  330.1 1.9 gather_fusion.1
  332.0 3.8 convolution_multiply_fusion.5
  335.8 9.2 %scatter_fusion.1 = f32[32,128,512]{2,1,0:T(8,128)} fusion(f32[32,128,512]{2,1,0:T(8,128)} %get-tuple-element.339, s32[16]{0:T(128)S(1)} %compare_select_fusion.9, f32[16,128,512]{2,1,0:T(8,128)} %convolution_multiply_fusion.5), kind=kCustom, calls=%fused_computation.3.clone.1 | custom fusion | flops 1048576 | bytes 12582976 | tf_op jit(solution)/shard_map/while/body/scatter-add | solution.py:57
  345.0 6.0 %convert_element_type.58 = bf16[32,128,512]{2,1,0:T(8,128)(2,1)} convert(f32[32,128,512]{2,1,0:T(8,128)} %get-tuple-element.101) | non-fusion elementwise | flops 2097152 | bytes 12582912 | tf_op jit(solution)/shard_map/convert_element_type | solution.py:109
  351.0 63.5 %psum.15 = f32[512]{0:T(512)S(1)} all-reduce(f32[512]{0:T(512)S(1)} %get-tuple-element.153), channel_id=1, replica_groups=mesh['row'=8,'col'=2,'rep'=2] {'row','col'}, use_global_device_ids=true, to_apply=%region_8.9 | all-reduce | flops 512 | bytes 4096 | tf_op jit(solution)/shard_map/psum | solution.py:96
  415.0 2.3 broadcast_multiply_fusion
  417.4 14.9 %reduce-scatter.5.cloned.1.call-done = bf16[512,512]{1,0:T(8,128)(2,1)} async-done(((bf16[4096,512]{1,0:T(8,128)(2,1)}), bf16[512,512]{1,0:T(8,128)(2,1)}) %reduce-scatter.5.cloned.1.call-update) | async-done | bytes 524304 | tf_op jit(solution)/shard_map/reduce_scatter | solution.py:108
  (49 shorter events, 6.1 us)
Async XLA Ops:
  7.2 211.6 %copy-start = (bf16[512,512]{1,0:T(8,128)(2,1)S(1)}, bf16[512,512]{1,0:T(8,128)(2,1)}, u32[]{:S(2)}) copy-start(bf16[512,512]{1,0:T(8,128)(2,1)} %param.13) | copy-start | bytes 1572868
  7.2 50.8 %all-gather.3.cloned.1.call-start = ((), (), s32[]{:S(2)}) async-start(), calls=%async_computation.2 | async-start | bytes 4718592 | tf_op jit(solution)/shard_map/all_gather | solution.py:77
  7.9 210.8 %reduce-scatter.3.cloned.1.call-start = ((), (), s32[]{:S(2)}) async-start(), calls=%async_computation.3 | async-start | bytes 1572864 | tf_op jit(solution)/shard_map/reduce_scatter | solution.py:82
  163.8 54.9 %copy-start.4 = (bf16[512,512]{1,0:T(8,128)(2,1)S(1)}, bf16[512,512]{1,0:T(8,128)(2,1)}, u32[]{:S(2)}) copy-start(bf16[512,512]{1,0:T(8,128)(2,1)} %param.19) | copy-start | bytes 1572868
  163.9 54.9 %copy-start.5 = (f32[512]{0:T(512)S(1)}, f32[512]{0:T(512)}, u32[]{:S(2)}) copy-start(f32[512]{0:T(512)} %param.14) | copy-start | bytes 6148
  165.0 79.2 %all-gather.5.cloned.1.call-start = ((), (), s32[]{:S(2)}) async-start(), calls=%async_computation.5 | async-start | bytes 1572864 | tf_op jit(solution)/shard_map/all_gather | solution.py:103
  222.7 192.3 %all-reduce.2.cloned.1.call-start = ((), (), s32[]{:S(2)}) async-start(), calls=%async_computation.4 | async-start | bytes 2097152 | tf_op jit(solution)/shard_map/psum | solution.py:96
  222.8 6.4 %copy-start.1 = (bf16[512,512]{1,0:T(8,128)(2,1)S(1)}, bf16[512,512]{1,0:T(8,128)(2,1)}, u32[]{:S(2)}) copy-start(bf16[512,512]{1,0:T(8,128)(2,1)} %reduce-scatter.3.cloned.1.call-done) | copy-start | bytes 1572868
  230.7 201.6 %reduce-scatter.5.cloned.1.call-start = ((), (), s32[]{:S(2)}) async-start(), calls=%async_computation.6 | async-start | bytes 4718592 | tf_op jit(solution)/shard_map/reduce_scatter | solution.py:108
  244.2 4.3 copy-start.2
  244.2 4.3 copy-start.3
Sparse Core Ops, SparseCore 0:
  9.6 48.3 all-gather.2
  165.1 53.5 reduce-scatter.2
  222.8 21.3 all-gather.4
  248.5 93.0 all-reduce.1
  351.1 81.0 reduce-scatter.4
where the time goes:
time: 443 us; the launch traced here: 439 us
  waiting for transfers between devices  130 us (29%)
  other arithmetic  119 us (27%)
  blocking collectives  63.5 us (14%)
  matrix products  55 us (12%)
  local copies, waits for them, and re-layouts  48 us (11%)
  between operations  15.7 us (4%)
  loops' own time  7.74 us (2%)
    psum x1, blocking collectives, on_device(): lax.psum((weight_local, bias_local), ('row', 'col'))  63.5 us
    scatter-add x6, other arithmetic, backward_step(): return accum.at[local].add(product * live[:, None, None])  54.3 us
    reduce_scatter x1, waiting for transfers between devices, on_device(): lax.psum_scatter(partial_value.reshape(row_tiles * edge, width).astype(jn...  53.7 us
    all_gather x1, waiting for transfers between devices, on_device(): column_block = lax.all_gather(features, 'row', axis=0, tiled=True)  46.9 us
    scatter-add x6, other arithmetic, forward_step(): return accum.at[row_group].add(product * live[:, None, None])  37 us
    dot_general x6, matrix products, forward_step(): jnp.einsum('gij,gjf->gif', tile_group, taken, preferred_element_type=jnp....  27 us
    gather x6, local copies, waits for them, and re-layouts, forward_step(): taken = jnp.take(blocks, local, axis=0)  25.6 us
    dot_general x6, matrix products, backward_step(): jnp.einsum('gji,gjf->gif', tile_group, taken, preferred_element_type=jnp....  22.6 us
  transfers between devices with their start and end apart: 5, of which 4 were waited for; matrix products, arithmetic and copies ran while one was open for 26% of the time, Pallas kernels for 0%

commit v1 on v0

--- a/solution.py
+++ b/solution.py
@@ -1,11 +1,15 @@
+import functools
 import math
 
 import jax
 import jax.numpy as jnp
 from jax import lax
+from jax.experimental import pallas as pl
+from jax.experimental.pallas import tpu as pltpu
 from jax.sharding import PartitionSpec as P
 
 slot_group = 16
+feature_chunks = 2
 
 
 def tile_range(cols_in, live_count, first_block, last_block):
@@ -114,6 +118,427 @@
     return (activated, weight_grad, bias_grad, feature_sum)
 
 
+MESH = pl.DeviceIdType.MESH
+
+
+def densify(tiles, rows_in, cols_in, live_count, row_tiles, col_tiles, wide):
+    slots, edge = tiles.shape[0], tiles.shape[-1]
+    per_step = wide // edge
+    steps = col_tiles // per_step
+
+    def body(rows_ref, cols_ref, count_ref, tiles_ref, out_ref, accum, cursor):
+        step = pl.program_id(0)
+
+        @pl.when(step == 0)
+        def _():
+            cursor[0] = 0
+
+        count = count_ref[0]
+        for part in range(per_step):
+            column = step * per_step + part
+            accum[...] = jnp.zeros_like(accum)
+
+            def more(slot):
+                return (slot < count) & (cols_ref[jnp.minimum(slot, slots - 1)] == column)
+
+            def add(slot):
+                window = pl.ds(pl.multiple_of(rows_ref[slot] * edge, edge), edge)
+                accum[window, :] += tiles_ref[slot].astype(jnp.float32)
+                return slot + 1
+
+            cursor[0] = lax.while_loop(more, add, cursor[0])
+            out_ref[0, :, part * edge : (part + 1) * edge] = accum[...].astype(jnp.bfloat16)
+
+    return pl.pallas_call(
+        body,
+        out_shape=jax.ShapeDtypeStruct((steps, row_tiles * edge, wide), jnp.bfloat16),
+        grid_spec=pltpu.PrefetchScalarGridSpec(
+            num_scalar_prefetch=3,
+            grid=(steps,),
+            in_specs=[
+                pl.BlockSpec(
+                    tiles.shape, lambda s, *_: (0, 0, 0), pipeline_mode=pl.Buffered(1)
+                )
+            ],
+            out_specs=pl.BlockSpec((1, row_tiles * edge, wide), lambda s, *_: (s, 0, 0)),
+            scratch_shapes=[
+                pltpu.VMEM((row_tiles * edge, edge), jnp.float32),
+                pltpu.SMEM((1,), jnp.int32),
+            ],
+        ),
+        compiler_params=pltpu.CompilerParams(vmem_limit_bytes=24 << 20),
+    )(rows_in, cols_in, live_count, tiles)
+
+
+def layer_kernel(
+    Z, FC, scale,
+    a_hbm, x_ref, w_ref, b_ref, cot_ref,
+    act_ref, wg_ref, bg_ref, fg_ref,
+    av, xg, acc, psend, precv, gath, dpre_s, dg,
+    own, sbuf, srecv, csend, crecv,
+    fsum, wl, wra, wa, wrb, wb, wrc, wfin, bs, br, br2,
+    a_sem, gz_s, gz_r, gs_s, gs_r, p_s, p_r, d_s, d_r,
+    s_s, s_r, c_s, c_r, w_s, w_r, wz_s, wz_r, wf_s, wf_r, bz_s, bz_r, bx_s, bx_r,
+):
+    r = lax.axis_index("row")
+    c = lax.axis_index("col")
+    z, k = r // 2, r % 2
+    V, F = x_ref.shape
+    fc = F // FC
+    f32, bf16 = jnp.float32, jnp.bfloat16
+    sib = {"row": z * 2 + (1 - k)}
+    peer = {"col": 1 - c}
+
+    def at_z(t):
+        return {"row": t * 2 + k}
+
+    def rc(src, dst, ss, rs, dev):
+        return pltpu.make_async_remote_copy(
+            src_ref=src, dst_ref=dst, send_sem=ss, recv_sem=rs, device_id=dev, device_id_type=MESH
+        )
+
+    def got(dst, rs):
+        rc(dst, dst, d_s.at[0], rs, sib).wait_recv()
+
+    for s in range(2 * Z):
+        pltpu.make_async_copy(a_hbm.at[s], av.at[s], a_sem.at[s]).start()
+
+    barrier = pltpu.get_barrier_semaphore()
+    pl.semaphore_signal(barrier, inc=1, device_id=sib, device_id_type=MESH)
+    pl.semaphore_signal(barrier, inc=1, device_id=peer, device_id_type=MESH)
+    for off in range(1, Z):
+        pl.semaphore_signal(barrier, inc=1, device_id=at_z((z + off) % Z), device_id_type=MESH)
+    for h in range(FC):
+        xg[h, z, k] = x_ref[:, h * fc : (h + 1) * fc]
+    pl.semaphore_wait(barrier, Z + 1)
+
+    def z_copy(h, t, step):
+        slot = xg.at[h, t, k]
+        return rc(slot, slot, gz_s.at[h, (1 - step) // 2, t], gz_r.at[h, t], at_z(z + step))
+
+    def s_copy(h, t):
+        slot = xg.at[h, t, k]
+        return rc(slot, slot, gs_s.at[h, t], gs_r.at[h, t], sib)
+
+    def own_sends(h):
+        @pl.when(z < Z - 1)
+        def _():
+            z_copy(h, z, 1).start()
+
+        @pl.when(z > 0)
+        def _():
+            z_copy(h, z, -1).start()
+
+        s_copy(h, z).start()
+
+    def mm(h, t, plane, first=False):
+        s = t * 2 + plane
+        if h == 0:
+            pltpu.make_async_copy(a_hbm.at[s], av.at[s], a_sem.at[s]).wait()
+        prod = jnp.dot(av[s], xg[h, t, plane], preferred_element_type=f32)
+        if first:
+            acc[h] = prod
+        else:
+            acc[h] += prod
+
+    def p_copy(h):
+        return rc(psend.at[h], precv.at[h], p_s.at[h], p_r.at[h], peer)
+
+    own_sends(0)
+    for h in range(FC):
+        mm(h, z, k, True)
+        got(xg.at[h, z, 1 - k], gs_r.at[h, z])
+        mm(h, z, 1 - k)
+        for dist in range(1, Z):
+            sides = ((z - dist, z - dist >= 0, 1), (z + dist, z + dist < Z, -1))
+            for t, valid, step in sides:
+
+                @pl.when(valid)
+                def _(t=t, step=step):
+                    got(xg.at[h, t, k], gz_r.at[h, t])
+
+                    @pl.when((z + step >= 0) & (z + step < Z))
+                    def _():
+                        z_copy(h, t, step).start()
+
+                    s_copy(h, t).start()
+
+            if dist == max(Z - 2, 1) and h + 1 < FC:
+                own_sends(h + 1)
+            for t, valid, step in sides:
+
+                @pl.when(valid)
+                def _(t=t):
+                    mm(h, t, k)
+                    got(xg.at[h, t, 1 - k], gs_r.at[h, t])
+                    mm(h, t, 1 - k)
+
+        psend[h] = acc[h, pl.ds(pl.multiple_of((1 - c) * V, V), V), :].astype(bf16)
+        p_copy(h).start()
+
+    pre = jnp.broadcast_to(b_ref[...], (V, F))
+    for h in range(FC):
+        p_copy(h).wait_recv()
+        g = acc[h, pl.ds(pl.multiple_of(c * V, V), V), :] + precv[h].astype(f32)
+        gath[:, h * fc : (h + 1) * fc] = g.astype(bf16)
+        pre = pre + jnp.dot(
+            g.astype(bf16), w_ref[h * fc : (h + 1) * fc, :], preferred_element_type=f32
+        )
+    sig = jax.nn.sigmoid(pre)
+    act_ref[...] = (pre * sig).astype(bf16)
+    dval = (cot_ref[...].astype(f32) * sig * (1.0 + pre * (1.0 - sig))).astype(bf16)
+    dpre_s[...] = dval
+
+    def d_copy(h):
+        slot = dg.at[h, c]
+        return rc(slot, slot, d_s.at[h], d_r.at[h], peer)
+
+    for h in range(FC):
+        dg[h, c] = lax.dot_general(
+            w_ref[h * fc : (h + 1) * fc, :], dpre_s[...], (((1,), (1,)), ((), ())),
+            preferred_element_type=f32,
+        ).astype(bf16)
+        d_copy(h).start()
+
+    bs[0] = jnp.sum(dpre_s[...].astype(f32).reshape(V // 8, 8, F), axis=0)
+    wl[...] = lax.dot_general(
+        gath[...], dpre_s[...], (((0,), (0,)), ((), ())), preferred_element_type=f32
+    )
+    H, Q, P8 = F // 2, F // 4, F // (4 * Z)
+    wa_copy = rc(wl.at[pl.ds(pl.multiple_of((1 - k) * H, H), H), :], wra, w_s.at[0], w_r.at[0], sib)
+    ba_copy = rc(bs.at[0], br.at[0], bx_s.at[0], bx_r.at[0], sib)
+    wb_copy = rc(wa.at[pl.ds(pl.multiple_of((1 - c) * Q, Q), Q), :], wrb, w_s.at[1], w_r.at[1], peer)
+    bb_copy = rc(bs.at[1], br.at[1], bx_s.at[1], bx_r.at[1], peer)
+    we_copy = rc(wfin.at[k, c], wfin.at[k, c], w_s.at[2], w_r.at[2], peer)
+    wf_copy = rc(wfin.at[k], wfin.at[k], w_s.at[3], w_r.at[3], sib)
+
+    def wc_copy(off):
+        t = (z + off) % Z
+        return rc(wb.at[t], wrc.at[off], wz_s.at[off], wz_r.at[off], at_z(t))
+
+    def wd_copy(off):
+        t = (z + off) % Z
+        return rc(wfin.at[k, c, z], wfin.at[k, c, z], wf_s.at[off], wf_r.at[off], at_z(t))
+
+    def bc_copy(off):
+        t = (z + off) % Z
+        return rc(bs.at[2], br2.at[off], bz_s.at[off], bz_r.at[off], at_z(t))
+
+    wa_copy.start()
+    ba_copy.start()
+
+    def stage_b():
+        wa_copy.wait_recv()
+        ba_copy.wait_recv()
+        wa[...] = wl[pl.ds(pl.multiple_of(k * H, H), H), :] + wra[...]
+        bs[1] = bs[0] + br[0]
+        wb_copy.start()
+        bb_copy.start()
+
+    def stage_c():
+        wb_copy.wait_recv()
+        bb_copy.wait_recv()
+        both = wa[pl.ds(pl.multiple_of(c * Q, Q), Q), :] + wrb[...]
+        wb[...] = both.astype(bf16).reshape(Z, P8, F)
+        bs[2] = bs[1] + br[1]
+        for off in range(1, Z):
+            wc_copy(off).start()
+            bc_copy(off).start()
+
+    def stage_d():
+        total = wb[z].astype(f32)
+        btotal = bs[2]
+        for off in range(1, Z):
+            wc_copy(off).wait_recv()
+            bc_copy(off).wait_recv()
+            total = total + wrc[off].astype(f32)
+            btotal = btotal + br2[off]
+        wfin[k, c, z] = (total * scale).astype(bf16)
+        bg_ref[...] = btotal * scale
+        for off in range(1, Z):
+            wd_copy(off).start()
+
+    def stage_e():
+        for off in range(1, Z):
+            t = (z - off + Z) % Z
+            got(wfin.at[k, c, t], wf_r.at[off])
+        we_copy.start()
+
+    def stage_f():
+        got(wfin.at[k, 1 - c], w_r.at[2])
+        wf_copy.start()
+
+    def s2_copy(h, d):
+        return rc(sbuf.at[h, d], srecv.at[h, d], s_s.at[h, d], s_r.at[h, d], sib)
+
+    def c_copy(h, d, way):
+        step = 1 if way == 0 else -1
+        return rc(
+            csend.at[h, d], crecv.at[h, d, way], c_s.at[h, d], c_r.at[h, d, way], at_z(z + step)
+        )
+
+    def bmm(h, d, plane):
+        s = d * 2 + plane
+        total = jnp.dot(dg[h, 0], av[s, :V, :], preferred_element_type=f32)
+        total = total + jnp.dot(dg[h, 1], av[s, V:, :], preferred_element_type=f32)
+        return total.astype(bf16)
+
+    def compute(h):
+        got(dg.at[h, 1 - c], d_r.at[h])
+
+        def one(i, carry):
+            d = jnp.where(z * 2 < Z, Z - 1 - i, i)
+            sbuf[h, d] = bmm(h, d, 1 - k)
+            s2_copy(h, d).start()
+            own[h, d] = bmm(h, d, k)
+            return carry
+
+        lax.fori_loop(0, Z, one, 0)
+
+    def local_sum(h, d):
+        s2_copy(h, d).wait_recv()
+        return own[h, d].astype(f32) + srecv[h, d].astype(f32)
+
+    def chain(h):
+        for dist in range(Z - 1, 0, -1):
+            for way, d, valid, inner in (
+                (0, z + dist, z + dist < Z, z > 0),
+                (1, z - dist, z - dist >= 0, z < Z - 1),
+            ):
+
+                @pl.when(valid & inner)
+                def _(way=way, d=d):
+                    total = local_sum(h, d)
+                    got(crecv.at[h, d, way], c_r.at[h, d, way])
+                    csend[h, d] = (total + crecv[h, d, way].astype(f32)).astype(bf16)
+                    c_copy(h, d, way).start()
+
+                @pl.when(valid & jnp.logical_not(inner))
+                def _(way=way, d=d):
+                    csend[h, d] = local_sum(h, d).astype(bf16)
+                    c_copy(h, d, way).start()
+
+    def finish(h):
+        s2_copy(h, z).wait_recv()
+        fsum[...] = own[h, z].astype(f32) + srecv[h, z].astype(f32)
+
+        @pl.when(z > 0)
+        def _():
+            got(crecv.at[h, z, 0], c_r.at[h, z, 0])
+            fsum[...] += crecv[h, z, 0].astype(f32)
+
+        @pl.when(z < Z - 1)
+        def _():
+            got(crecv.at[h, z, 1], c_r.at[h, z, 1])
+            fsum[...] += crecv[h, z, 1].astype(f32)
+
+        fg_ref[:, h * fc : (h + 1) * fc] = fsum[...].T.astype(bf16)
+
+    compute(0)
+    stage_b()
+    for h in range(1, FC):
+        compute(h)
+    stage_c()
+    chain(0)
+    stage_d()
+    for h in range(1, FC):
+        chain(h)
+    stage_e()
+    for h in range(FC - 1):
+        finish(h)
+    stage_f()
+    finish(FC - 1)
+    got(wfin.at[1 - k], w_r.at[3])
+    wg_ref[...] = wfin[...].astype(f32).reshape(F, F)
+
+    for h in range(FC):
+        for t in range(Z):
+
+            @pl.when((z < Z - 1) & (t <= z))
+            def _(t=t):
+                z_copy(h, t, 1).wait_send()
+
+            @pl.when((z > 0) & (t >= z))
+            def _(t=t):
+                z_copy(h, t, -1).wait_send()
+
+            s_copy(h, t).wait_send()
+            s2_copy(h, t).wait_send()
+
+            @pl.when(t > z)
+            def _(t=t):
+                c_copy(h, t, 0).wait_send()
+
+            @pl.when(t < z)
+            def _(t=t):
+                c_copy(h, t, 1).wait_send()
+
+        p_copy(h).wait_send()
+        d_copy(h).wait_send()
+    for copy in (wa_copy, ba_copy, wb_copy, bb_copy, we_copy, wf_copy):
+        copy.wait_send()
+    for off in range(1, Z):
+        wc_copy(off).wait_send()
+        bc_copy(off).wait_send()
+        wd_copy(off).wait_send()
+
+
+def fused_layer(adjacency, features, weights, bias_vector, cotangent, Z, FC):
+    V, F = features.shape
+    R, fc = 2 * Z, F // FC
+    f32, bf16 = jnp.float32, jnp.bfloat16
+    H, Q, P8 = F // 2, F // 4, F // (4 * Z)
+    dma = pltpu.SemaphoreType.DMA
+    vm = pltpu.VMEM
+    scale = 1.0 / math.sqrt(V * R * 2)
+    whole = pl.BlockSpec(memory_space=pltpu.VMEM)
+    return pl.pallas_call(
+        functools.partial(layer_kernel, Z, FC, scale),
+        out_shape=(
+            jax.ShapeDtypeStruct((V, F), bf16),
+            jax.ShapeDtypeStruct((F, F), f32),
+            jax.ShapeDtypeStruct((8, F), f32),
+            jax.ShapeDtypeStruct((V, F), bf16),
+        ),
+        in_specs=[pl.BlockSpec(memory_space=pl.ANY)] + [whole] * 4,
+        out_specs=[whole] * 4,
+        scratch_shapes=[
+            vm((R, 2 * V, V), bf16), vm((FC, Z, 2, V, fc), bf16), vm((FC, 2 * V, fc), f32),
+            vm((FC, V, fc), bf16), vm((FC, V, fc), bf16), vm((V, F), bf16), vm((V, F), bf16),
+            vm((FC, 2, fc, V), bf16),
+            vm((FC, Z, fc, V), bf16), vm((FC, Z, fc, V), bf16), vm((FC, Z, fc, V), bf16),
+            vm((FC, Z, fc, V), bf16), vm((FC, Z, 2, fc, V), bf16),
+            vm((fc, V), f32), vm((F, F), f32), vm((H, F), f32), vm((H, F), f32), vm((Q, F), f32),
+            vm((Z, P8, F), bf16), vm((Z, P8, F), bf16), vm((2, 2, Z, P8, F), bf16),
+            vm((3, 8, F), f32), vm((2, 8, F), f32), vm((Z, 8, F), f32),
+            dma((R,)), dma((FC, 2, Z)), dma((FC, Z)), dma((FC, Z)), dma((FC, Z)),
+            dma((FC,)), dma((FC,)), dma((FC,)), dma((FC,)),
+            dma((FC, Z)), dma((FC, Z)), dma((FC, Z)), dma((FC, Z, 2)),
+            dma((4,)), dma((4,)), dma((Z,)), dma((Z,)), dma((Z,)), dma((Z,)),
+            dma((Z,)), dma((Z,)), dma((2,)), dma((2,)),
+        ],
+        compiler_params=pltpu.CompilerParams(
+            collective_id=0, has_side_effects=True, vmem_limit_bytes=60 << 20
+        ),
+    )(adjacency, features, weights, bias_vector.reshape(1, F), cotangent)
+
+
+def on_device_fused(
+    features, weights, bias_vector, tile_values, tile_rows, tile_cols, tile_counts, cotangent
+):
+    tiles = tile_values[0, 0]
+    rows = lax.axis_size("row")
+    local_rows, edge = features.shape[0], tiles.shape[-1]
+    adjacency = densify(
+        tiles, tile_rows[0, 0], tile_cols[0, 0], tile_counts[0],
+        local_rows * 2 // edge, local_rows * rows // edge, local_rows,
+    )
+    activated, weight_grad, bias_rows, feature_grad = fused_layer(
+        adjacency, features, weights, bias_vector, cotangent, rows // 2, feature_chunks
+    )
+    return (activated, weight_grad, jnp.sum(bias_rows, axis=0), feature_grad)
+
+
 def solution(mesh):
     in_specs = (
         P(("rep", "col", "row"), None),
@@ -131,6 +556,7 @@
         P("rep"),
         P(("rep", "col", "row"), None),
     )
+    small = mesh.shape["col"] == 2 and mesh.shape["row"] % 2 == 0
     return jax.shard_map(
-        on_device, mesh=mesh, in_specs=in_specs, out_specs=out_specs, check_vma=False
-    )
+        on_device_fused if small else on_device, mesh=mesh, in_specs=in_specs, out_specs=out_specs, check_vma=False
+    )

time: 443 us -> 138 us (0.31)
  waiting for transfers between devices: 130 us -> 0 us
  Pallas kernels: 0 us -> 121 us
  other arithmetic: 119 us -> 1.31 us
  blocking collectives: 63.5 us -> 0 us
  matrix products: 55 us -> 0 us
  local copies, waits for them, and re-layouts: 48 us -> 12.7 us
  between operations: 15.7 us -> 1.32 us
  loops' own time: 7.74 us -> 0 us
    pallas_call x0 -> x2, Pallas kernels: none -> 121 us  [the longest x1 118 us: fused_layer(): pl.pallas_call(functools.partial(layer_kernel, Z, FC, scale), out_shape=(...]
    scatter-add x12 -> x0, other arithmetic: 91.2 us -> none  [the longest x6 54.3 us: backward_step(): return accum.at[local].add(product * live[:, None, None])]
    reduce_scatter x2 -> x0, waiting for transfers between devices: 68.6 us -> none  [the longest x1 53.7 us: on_device(): lax.psum_scatter(partial_value.reshape(row_tiles * edge, width).astype(jn...]
    psum x1 -> x0, blocking collectives: 63.5 us -> none  [on_device(): lax.psum((weight_local, bias_local), ('row', 'col'))]
    all_gather x2 -> x0, waiting for transfers between devices: 60.4 us -> none  [the longest x1 46.9 us: on_device(): column_block = lax.all_gather(features, 'row', axis=0, tiled=True)]
    dot_general x15 -> x0, matrix products: 55 us -> none  [the longest x6 27 us: forward_step(): jnp.einsum('gij,gjf->gif', tile_group, taken, preferred_element_type=jnp....]
    gather x12 -> x0, local copies, waits for them, and re-layouts: 37 us -> none  [the longest x6 25.6 us: forward_step(): taken = jnp.take(blocks, local, axis=0)]
    and x12 -> x0, other arithmetic: 11.5 us -> none  [the longest x6 7.71 us: forward_step(): taken = jnp.take(blocks, local, axis=0)]
  transfers between devices with their start and end apart: 5 -> 0, of which waited for: 4 -> 0; matrix products, arithmetic and copies ran while one was open for 26% -> 0% of each run, Pallas kernels for 0% -> 0%
where the time goes in v1:
time: 138 us; the launch traced here: 137 us
  Pallas kernels  121 us (88%)
  local copies, waits for them, and re-layouts  12.7 us (9%)
    pallas_call x1, Pallas kernels, fused_layer(): pl.pallas_call(functools.partial(layer_kernel, Z, FC, scale), out_shape=(...  118 us
    unnamed x11, local copies, waits for them, and re-layouts  12.7 us
    pallas_call x1, Pallas kernels, densify(): pl.pallas_call(body, out_shape=jax.ShapeDtypeStruct((steps, row_tiles * e...  2.92 us

profile of v1, /device:TPU:4, one launch (start us, length us, event | category | flops | bytes accessed | tf_op | source)
XLA Modules:
  0.0 136.6 jit_solution(317752210117364071)
XLA Ops:
  1.3 0.0 copy-start.1
  1.3 2.2 %copy-done.1 = bf16[1,1,128,128,128]{4,3,2,1,0:T(8,128)(2,1)S(1)} copy-done((bf16[1,1,128,128,128]{4,3,2,1,0:T(8,128)(2,1)S(1)}, bf16[1,1,128,128,128]{4,3,2,1,0:T(8,128)(2,1)}, u32[]{:S(2)}) %copy-start.1) | copy-done | bytes 4194328
  3.5 0.0 copy-start.2
  3.5 0.7 copy-done.2
  4.1 0.0 copy-start.3
  4.1 0.7 copy-done.3
  4.8 2.9 %shard_map.111.a_hbm = bf16[8,1024,512]{2,1,0:T(8,128)(2,1)S(1)} custom-call(s32[128]{0:T(128)S(1)} %bitcast.7, s32[128]{0:T(128)S(1)} %bitcast.8, s32[1]{0:T(128)} %bitcast.5.count_ref, bf16[128,128,128]{2,1,0:T(8,128)(2,1)S(1)} %bitcast.6), custom_call_target="tpu_custom_call" | custom-call | tf_op jit(solution)/shard_map/pallas_call | solution.py:152
  7.7 0.0 copy-start
  7.7 3.2 %copy-done = bf16[8,1024,512]{2,1,0:T(8,128)(2,1)} copy-done((bf16[8,1024,512]{2,1,0:T(8,128)(2,1)}, bf16[8,1024,512]{2,1,0:T(8,128)(2,1)S(1)}, u32[]{:S(2)}) %copy-start) | copy-done | bytes 8388632
  10.9 118.4 %shard_map.112 = (bf16[512,512]{1,0:T(8,128)(2,1)}, f32[512,512]{1,0:T(8,128)}, f32[8,512]{1,0:T(8,128)}, bf16[512,512]{1,0:T(8,128)(2,1)}) custom-call(bf16[8,1024,512]{2,1,0:T(8,128)(2,1)} %copy-done, bf16[512,512]{1,0:T(8,128)(2,1)} %x_ref.1, bf16[512,512]{1,0:T(8,128)(2,1)} %w_ref.1, f32[1,512]{1,0:T(1,128)} %bitcast.9, bf16[512,512]{1,0:T(8,128)(2,1)} %cot_ref.1), custom_call_target="tpu_custom_call" | custom-call | tf_op jit(solution)/shard_map/pallas_call | solution.py:495
  129.3 1.3 reduce_sum.9
  130.6 1.9 %copy.16 = bf16[512,512]{1,0:T(8,128)(2,1)} copy(bf16[512,512]{1,0:T(8,128)(2,1)} %get-tuple-element.16) | data formatting | bytes 1048576
  132.5 2.3 %copy.17 = f32[512,512]{1,0:T(8,128)} copy(f32[512,512]{1,0:T(8,128)} %get-tuple-element.17) | data formatting | bytes 2097152
  134.7 1.9 %copy.18 = bf16[512,512]{1,0:T(8,128)(2,1)} copy(bf16[512,512]{1,0:T(8,128)(2,1)} %get-tuple-element.19) | data formatting | bytes 1048576
Async XLA Ops:
  1.3 2.2 %copy-start.1 = (bf16[1,1,128,128,128]{4,3,2,1,0:T(8,128)(2,1)S(1)}, bf16[1,1,128,128,128]{4,3,2,1,0:T(8,128)(2,1)}, u32[]{:S(2)}) copy-start(bf16[1,1,128,128,128]{4,3,2,1,0:T(8,128)(2,1)} %param.11) | copy-start | bytes 12582916
  3.5 0.7 copy-start.2
  4.1 0.7 copy-start.3
  7.7 3.2 %copy-start = (bf16[8,1024,512]{2,1,0:T(8,128)(2,1)}, bf16[8,1024,512]{2,1,0:T(8,128)(2,1)S(1)}, u32[]{:S(2)}) copy-start(bf16[8,1024,512]{2,1,0:T(8,128)(2,1)S(1)} %shard_map.111.a_hbm) | copy-start | bytes 25165828

commit v2 on v1

--- a/solution.py
+++ b/solution.py
@@ -126,14 +126,25 @@
     per_step = wide // edge
     steps = col_tiles // per_step
 
-    def body(rows_ref, cols_ref, count_ref, tiles_ref, out_ref, accum, cursor):
+    pieces = slots // slot_group
+
+    def body(rows_ref, cols_ref, count_ref, tiles_hbm, out_ref, tiles_ref, accum, cursor, sems):
         step = pl.program_id(0)
+        count = count_ref[0]
+
+        def piece_copy(piece):
+            window = pl.ds(piece * slot_group, slot_group)
+            return pltpu.make_async_copy(tiles_hbm.at[window], tiles_ref.at[window], sems.at[piece])
 
         @pl.when(step == 0)
         def _():
             cursor[0] = 0
-
-        count = count_ref[0]
+            for piece in range(pieces):
+
+                @pl.when(piece * slot_group < count)
+                def _(piece=piece):
+                    piece_copy(piece).start()
+
         for part in range(per_step):
             column = step * per_step + part
             accum[...] = jnp.zeros_like(accum)
@@ -142,6 +153,10 @@
                 return (slot < count) & (cols_ref[jnp.minimum(slot, slots - 1)] == column)
 
             def add(slot):
+                @pl.when(slot % slot_group == 0)
+                def _():
+                    piece_copy(slot // slot_group).wait()
+
                 window = pl.ds(pl.multiple_of(rows_ref[slot] * edge, edge), edge)
                 accum[window, :] += tiles_ref[slot].astype(jnp.float32)
                 return slot + 1
@@ -155,18 +170,16 @@
         grid_spec=pltpu.PrefetchScalarGridSpec(
             num_scalar_prefetch=3,
             grid=(steps,),
-            in_specs=[
-                pl.BlockSpec(
-                    tiles.shape, lambda s, *_: (0, 0, 0), pipeline_mode=pl.Buffered(1)
-                )
-            ],
+            in_specs=[pl.BlockSpec(memory_space=pltpu.HBM)],
             out_specs=pl.BlockSpec((1, row_tiles * edge, wide), lambda s, *_: (s, 0, 0)),
             scratch_shapes=[
+                pltpu.VMEM(tiles.shape, tiles.dtype),
                 pltpu.VMEM((row_tiles * edge, edge), jnp.float32),
                 pltpu.SMEM((1,), jnp.int32),
+                pltpu.SemaphoreType.DMA((pieces,)),
             ],
         ),
-        compiler_params=pltpu.CompilerParams(vmem_limit_bytes=24 << 20),
+        compiler_params=pltpu.CompilerParams(vmem_limit_bytes=12 << 20),
     )(rows_in, cols_in, live_count, tiles)
 
 
@@ -175,10 +188,10 @@
     a_hbm, x_ref, w_ref, b_ref, cot_ref,
     act_ref, wg_ref, bg_ref, fg_ref,
     av, xg, acc, psend, precv, gath, dpre_s, dg,
-    own, sbuf, srecv, csend, crecv,
-    fsum, wl, wra, wa, wrb, wb, wrc, wfin, bs, br, br2,
+    own, sbuf, srecv, csend, crecv, cmid,
+    fsum, wl, wra, wa, wab, wrb, wb, wrc, wfin, bs, br, br2,
     a_sem, gz_s, gz_r, gs_s, gs_r, p_s, p_r, d_s, d_r,
-    s_s, s_r, c_s, c_r, w_s, w_r, wz_s, wz_r, wf_s, wf_r, bz_s, bz_r, bx_s, bx_r,
+    s_s, s_r, c_s, c_r, m_r, w_s, w_r, wz_s, wz_r, wf_s, wf_r, bz_s, bz_r, bx_s, bx_r,
 ):
     r = lax.axis_index("row")
     c = lax.axis_index("col")
@@ -212,23 +225,32 @@
         xg[h, z, k] = x_ref[:, h * fc : (h + 1) * fc]
     pl.semaphore_wait(barrier, Z + 1)
 
-    def z_copy(h, t, step):
+    end = (z == 0) | (z == Z - 1)
+
+    def mirrored(position):
+        return jnp.where(z * 2 < Z, position, Z - 1 - position)
+
+    def z_copy(h, t, dst, kind):
         slot = xg.at[h, t, k]
-        return rc(slot, slot, gz_s.at[h, (1 - step) // 2, t], gz_r.at[h, t], at_z(z + step))
+        return rc(slot, slot, gz_s.at[h, kind, dst], gz_r.at[h, t], at_z(dst))
 
     def s_copy(h, t):
         slot = xg.at[h, t, k]
         return rc(slot, slot, gs_s.at[h, t], gs_r.at[h, t], sib)
 
+    def own_targets(h, act):
+        @pl.when(end)
+        def _():
+            for position in (3, 2, 1):
+                act(z_copy(h, z, mirrored(position), 0))
+
+        @pl.when(jnp.logical_not(end))
+        def _():
+            for position in (2, 0):
+                act(z_copy(h, z, mirrored(position), 0))
+
     def own_sends(h):
-        @pl.when(z < Z - 1)
-        def _():
-            z_copy(h, z, 1).start()
-
-        @pl.when(z > 0)
-        def _():
-            z_copy(h, z, -1).start()
-
+        own_targets(h, lambda copy: copy.start())
         s_copy(h, z).start()
 
     def mm(h, t, plane, first=False):
@@ -249,29 +271,21 @@
         mm(h, z, k, True)
         got(xg.at[h, z, 1 - k], gs_r.at[h, z])
         mm(h, z, 1 - k)
-        for dist in range(1, Z):
-            sides = ((z - dist, z - dist >= 0, 1), (z + dist, z + dist < Z, -1))
-            for t, valid, step in sides:
-
-                @pl.when(valid)
-                def _(t=t, step=step):
-                    got(xg.at[h, t, k], gz_r.at[h, t])
-
-                    @pl.when((z + step >= 0) & (z + step < Z))
-                    def _():
-                        z_copy(h, t, step).start()
-
-                    s_copy(h, t).start()
-
-            if dist == max(Z - 2, 1) and h + 1 < FC:
+        for turn in range(Z - 1):
+            t = mirrored(jnp.where(end, (1, 3, 2)[turn], (2, 0, 3)[turn]))
+            got(xg.at[h, t, k], gz_r.at[h, t])
+            if turn == 0:
+
+                @pl.when(jnp.logical_not(end))
+                def _(t=t):
+                    z_copy(h, t, mirrored(0), 1).start()
+
+            s_copy(h, t).start()
+            if turn == 0 and h + 1 < FC:
                 own_sends(h + 1)
-            for t, valid, step in sides:
-
-                @pl.when(valid)
-                def _(t=t):
-                    mm(h, t, k)
-                    got(xg.at[h, t, 1 - k], gs_r.at[h, t])
-                    mm(h, t, 1 - k)
+            mm(h, t, k)
+            got(xg.at[h, t, 1 - k], gs_r.at[h, t])
+            mm(h, t, 1 - k)
 
         psend[h] = acc[h, pl.ds(pl.multiple_of((1 - c) * V, V), V), :].astype(bf16)
         p_copy(h).start()
@@ -307,7 +321,7 @@
     H, Q, P8 = F // 2, F // 4, F // (4 * Z)
     wa_copy = rc(wl.at[pl.ds(pl.multiple_of((1 - k) * H, H), H), :], wra, w_s.at[0], w_r.at[0], sib)
     ba_copy = rc(bs.at[0], br.at[0], bx_s.at[0], bx_r.at[0], sib)
-    wb_copy = rc(wa.at[pl.ds(pl.multiple_of((1 - c) * Q, Q), Q), :], wrb, w_s.at[1], w_r.at[1], peer)
+    wb_copy = rc(wab, wrb, w_s.at[1], w_r.at[1], peer)
     bb_copy = rc(bs.at[1], br.at[1], bx_s.at[1], bx_r.at[1], peer)
     we_copy = rc(wfin.at[k, c], wfin.at[k, c], w_s.at[2], w_r.at[2], peer)
     wf_copy = rc(wfin.at[k], wfin.at[k], w_s.at[3], w_r.at[3], sib)
@@ -331,6 +345,7 @@
         wa_copy.wait_recv()
         ba_copy.wait_recv()
         wa[...] = wl[pl.ds(pl.multiple_of(k * H, H), H), :] + wra[...]
+        wab[...] = wa[pl.ds(pl.multiple_of((1 - c) * Q, Q), Q), :].astype(bf16)
         bs[1] = bs[0] + br[0]
         wb_copy.start()
         bb_copy.start()
@@ -338,7 +353,7 @@
     def stage_c():
         wb_copy.wait_recv()
         bb_copy.wait_recv()
-        both = wa[pl.ds(pl.multiple_of(c * Q, Q), Q), :] + wrb[...]
+        both = wa[pl.ds(pl.multiple_of(c * Q, Q), Q), :] + wrb[...].astype(f32)
         wb[...] = both.astype(bf16).reshape(Z, P8, F)
         bs[2] = bs[1] + br[1]
         for off in range(1, Z):
@@ -354,7 +369,7 @@
             total = total + wrc[off].astype(f32)
             btotal = btotal + br2[off]
         wfin[k, c, z] = (total * scale).astype(bf16)
-        bg_ref[...] = btotal * scale
+        bg_ref[...] = jnp.sum(btotal, axis=0, keepdims=True) * scale
         for off in range(1, Z):
             wd_copy(off).start()
 
@@ -371,10 +386,12 @@
     def s2_copy(h, d):
         return rc(sbuf.at[h, d], srecv.at[h, d], s_s.at[h, d], s_r.at[h, d], sib)
 
-    def c_copy(h, d, way):
-        step = 1 if way == 0 else -1
+    def c_copy(h, d):
+        return rc(csend.at[h, d], crecv.at[h, z], c_s.at[h, d], c_r.at[h, z], at_z(d))
+
+    def mid_copy(h):
         return rc(
-            csend.at[h, d], crecv.at[h, d, way], c_s.at[h, d], c_r.at[h, d, way], at_z(z + step)
+            csend.at[h, Z - 1 - z], cmid.at[h], c_s.at[h, Z - 1 - z], m_r.at[h], at_z(mirrored(1))
         )
 
     def bmm(h, d, plane):
@@ -383,95 +400,95 @@
         total = total + jnp.dot(dg[h, 1], av[s, V:, :], preferred_element_type=f32)
         return total.astype(bf16)
 
-    def compute(h):
-        got(dg.at[h, 1 - c], d_r.at[h])
-
-        def one(i, carry):
-            d = jnp.where(z * 2 < Z, Z - 1 - i, i)
+    def target(i):
+        return mirrored(jnp.where(end, Z - 1 - i, (i + 2) % Z))
+
+    def local_sum(h, d):
+        s2_copy(h, d).wait_recv()
+        return own[h, d].astype(f32) + srecv[h, d].astype(f32)
+
+    def ship(h, i):
+        d = target(i)
+
+        @pl.when(end | (i != 1))
+        def _():
+            csend[h, d] = local_sum(h, d).astype(bf16)
+
+        @pl.when(end & (i == 0))
+        def _():
+            mid_copy(h).start()
+
+        @pl.when((end & (i != 0)) | (jnp.logical_not(end) & (i != 1)))
+        def _():
+            c_copy(h, d).start()
+
+    def products(i, carry):
+        d = target(i)
+        for h in range(FC):
+
+            @pl.when(i == 0)
+            def _(h=h):
+                got(dg.at[h, 1 - c], d_r.at[h])
+
             sbuf[h, d] = bmm(h, d, 1 - k)
             s2_copy(h, d).start()
             own[h, d] = bmm(h, d, k)
-            return carry
-
-        lax.fori_loop(0, Z, one, 0)
-
-    def local_sum(h, d):
-        s2_copy(h, d).wait_recv()
-        return own[h, d].astype(f32) + srecv[h, d].astype(f32)
-
-    def chain(h):
-        for dist in range(Z - 1, 0, -1):
-            for way, d, valid, inner in (
-                (0, z + dist, z + dist < Z, z > 0),
-                (1, z - dist, z - dist >= 0, z < Z - 1),
-            ):
-
-                @pl.when(valid & inner)
-                def _(way=way, d=d):
-                    total = local_sum(h, d)
-                    got(crecv.at[h, d, way], c_r.at[h, d, way])
-                    csend[h, d] = (total + crecv[h, d, way].astype(f32)).astype(bf16)
-                    c_copy(h, d, way).start()
-
-                @pl.when(valid & jnp.logical_not(inner))
-                def _(way=way, d=d):
-                    csend[h, d] = local_sum(h, d).astype(bf16)
-                    c_copy(h, d, way).start()
+
+            @pl.when(i > 0)
+            def _(h=h):
+                ship(h, i - 1)
+
+        return carry
+
+    def middle(h):
+        @pl.when(jnp.logical_not(end))
+        def _():
+            d = target(1)
+            got(cmid.at[h], m_r.at[h])
+            csend[h, d] = (local_sum(h, d) + cmid[h].astype(f32)).astype(bf16)
+            c_copy(h, d).start()
 
     def finish(h):
         s2_copy(h, z).wait_recv()
         fsum[...] = own[h, z].astype(f32) + srecv[h, z].astype(f32)
 
-        @pl.when(z > 0)
-        def _():
-            got(crecv.at[h, z, 0], c_r.at[h, z, 0])
-            fsum[...] += crecv[h, z, 0].astype(f32)
-
-        @pl.when(z < Z - 1)
-        def _():
-            got(crecv.at[h, z, 1], c_r.at[h, z, 1])
-            fsum[...] += crecv[h, z, 1].astype(f32)
+        for src in range(Z):
+
+            @pl.when((z != src) & jnp.logical_not(end & (z == Z - 1 - src)))
+            def _(src=src):
+                got(crecv.at[h, src], c_r.at[h, src])
+                fsum[...] += crecv[h, src].astype(f32)
 
         fg_ref[:, h * fc : (h + 1) * fc] = fsum[...].T.astype(bf16)
 
-    compute(0)
+    lax.fori_loop(0, Z, products, 0)
     stage_b()
-    for h in range(1, FC):
-        compute(h)
+    for h in range(FC):
+        middle(h)
     stage_c()
-    chain(0)
-    stage_d()
-    for h in range(1, FC):
-        chain(h)
-    stage_e()
     for h in range(FC - 1):
         finish(h)
+    stage_d()
+    stage_e()
+    finish(FC - 1)
     stage_f()
-    finish(FC - 1)
     got(wfin.at[1 - k], w_r.at[3])
-    wg_ref[...] = wfin[...].astype(f32).reshape(F, F)
+    wg_ref[...] = wfin[...].reshape(F, F)
 
     for h in range(FC):
+        own_targets(h, lambda copy: copy.wait_send())
+
+        @pl.when(jnp.logical_not(end))
+        def _(h=h):
+            z_copy(h, mirrored(2), mirrored(0), 1).wait_send()
+
         for t in range(Z):
-
-            @pl.when((z < Z - 1) & (t <= z))
-            def _(t=t):
-                z_copy(h, t, 1).wait_send()
-
-            @pl.when((z > 0) & (t >= z))
-            def _(t=t):
-                z_copy(h, t, -1).wait_send()
-
             s_copy(h, t).wait_send()
             s2_copy(h, t).wait_send()
 
-            @pl.when(t > z)
-            def _(t=t):
-                c_copy(h, t, 0).wait_send()
-
-            @pl.when(t < z)
-            def _(t=t):
-                c_copy(h, t, 1).wait_send()
+            @pl.when(z != t)
+            def _(h=h, t=t):
+                c_copy(h, t).wait_send()
 
         p_copy(h).wait_send()
         d_copy(h).wait_send()
@@ -496,8 +513,8 @@
         functools.partial(layer_kernel, Z, FC, scale),
         out_shape=(
             jax.ShapeDtypeStruct((V, F), bf16),
-            jax.ShapeDtypeStruct((F, F), f32),
-            jax.ShapeDtypeStruct((8, F), f32),
+            jax.ShapeDtypeStruct((F, F), bf16),
+            jax.ShapeDtypeStruct((1, F), f32),
             jax.ShapeDtypeStruct((V, F), bf16),
         ),
         in_specs=[pl.BlockSpec(memory_space=pl.ANY)] + [whole] * 4,
@@ -507,18 +524,18 @@
             vm((FC, V, fc), bf16), vm((FC, V, fc), bf16), vm((V, F), bf16), vm((V, F), bf16),
             vm((FC, 2, fc, V), bf16),
             vm((FC, Z, fc, V), bf16), vm((FC, Z, fc, V), bf16), vm((FC, Z, fc, V), bf16),
-            vm((FC, Z, fc, V), bf16), vm((FC, Z, 2, fc, V), bf16),
-            vm((fc, V), f32), vm((F, F), f32), vm((H, F), f32), vm((H, F), f32), vm((Q, F), f32),
+            vm((FC, Z, fc, V), bf16), vm((FC, Z, fc, V), bf16), vm((FC, fc, V), bf16),
+            vm((fc, V), f32), vm((F, F), f32), vm((H, F), f32), vm((H, F), f32), vm((Q, F), bf16), vm((Q, F), bf16),
             vm((Z, P8, F), bf16), vm((Z, P8, F), bf16), vm((2, 2, Z, P8, F), bf16),
             vm((3, 8, F), f32), vm((2, 8, F), f32), vm((Z, 8, F), f32),
             dma((R,)), dma((FC, 2, Z)), dma((FC, Z)), dma((FC, Z)), dma((FC, Z)),
             dma((FC,)), dma((FC,)), dma((FC,)), dma((FC,)),
-            dma((FC, Z)), dma((FC, Z)), dma((FC, Z)), dma((FC, Z, 2)),
+            dma((FC, Z)), dma((FC, Z)), dma((FC, Z)), dma((FC, Z)), dma((FC,)),
             dma((4,)), dma((4,)), dma((Z,)), dma((Z,)), dma((Z,)), dma((Z,)),
             dma((Z,)), dma((Z,)), dma((2,)), dma((2,)),
         ],
         compiler_params=pltpu.CompilerParams(
-            collective_id=0, has_side_effects=True, vmem_limit_bytes=60 << 20
+            collective_id=0, has_side_effects=True, vmem_limit_bytes=42 << 20
         ),
     )(adjacency, features, weights, bias_vector.reshape(1, F), cotangent)
 
@@ -536,7 +553,7 @@
     activated, weight_grad, bias_rows, feature_grad = fused_layer(
         adjacency, features, weights, bias_vector, cotangent, rows // 2, feature_chunks
     )
-    return (activated, weight_grad, jnp.sum(bias_rows, axis=0), feature_grad)
+    return (activated, weight_grad.astype(jnp.float32), bias_rows[0], feature_grad)
 
 
 def solution(mesh):
@@ -556,7 +573,7 @@
         P("rep"),
         P(("rep", "col", "row"), None),
     )
-    small = mesh.shape["col"] == 2 and mesh.shape["row"] % 2 == 0
+    small = mesh.shape["col"] == 2 and mesh.shape["row"] == 8
     return jax.shard_map(
         on_device_fused if small else on_device, mesh=mesh, in_specs=in_specs, out_specs=out_specs, check_vma=False
     )

time: 138 us -> 135 us (0.978)
  local copies, waits for them, and re-layouts: 12.7 us -> 5.67 us
  Pallas kernels: 121 us -> 126 us
    unnamed x11 -> x17, local copies, waits for them, and re-layouts: 12.7 us -> 5.67 us
    pallas_call x1, Pallas kernels: 118 us -> 123 us  [fused_layer(): pl.pallas_call(functools.partial(layer_kernel, Z, FC, scale), out_shape=(...]
where the time goes in v2:
time: 135 us; the launch traced here: 134 us
  Pallas kernels  126 us (93%)
  local copies, waits for them, and re-layouts  5.67 us (4%)
  between operations  1.36 us (1%)
    pallas_call x1, Pallas kernels, fused_layer(): pl.pallas_call(functools.partial(layer_kernel, Z, FC, scale), out_shape=(...  123 us
    unnamed x17, local copies, waits for them, and re-layouts  5.67 us
    pallas_call x1, Pallas kernels, densify(): pl.pallas_call(body, out_shape=jax.ShapeDtypeStruct((steps, row_tiles * e...  3.16 us

profile of v2, /device:TPU:4, one launch (start us, length us, event | category | flops | bytes accessed | tf_op | source)
XLA Modules:
  0.0 133.9 jit_solution(12005819580027985325)
XLA Ops:
  0.6 0.0 copy-start.4
  1.3 0.0 copy-start
  1.3 2.2 %copy-done = bf16[1,1,128,128,128]{4,3,2,1,0:T(8,128)(2,1)S(1)} copy-done((bf16[1,1,128,128,128]{4,3,2,1,0:T(8,128)(2,1)S(1)}, bf16[1,1,128,128,128]{4,3,2,1,0:T(8,128)(2,1)}, u32[]{:S(2)}) %copy-start) | copy-done | bytes 4194328
  3.5 0.0 copy-start.5
  3.5 0.7 copy-done.5
  4.1 0.0 copy-start.6
  4.1 0.7 copy-done.6
  4.8 0.0 copy-start.1
  4.8 0.0 copy-start.2
  4.8 0.0 copy-start.3
  4.8 3.2 %shard_map.111.a_hbm = bf16[8,1024,512]{2,1,0:T(8,128)(2,1)S(1)} custom-call(s32[128]{0:T(128)S(1)} %bitcast.10, s32[128]{0:T(128)S(1)} %bitcast.11, s32[1]{0:T(128)} %bitcast.6.count_ref, bf16[128,128,128]{2,1,0:T(8,128)(2,1)S(1)} %bitcast.7), custom_call_target="tpu_custom_call" | custom-call | tf_op jit(solution)/shard_map/pallas_call | solution.py:167
  8.0 0.0 copy-done.4
  8.0 0.0 copy-done.1
  8.0 0.0 copy-done.2
  8.0 0.0 copy-done.3
  8.0 122.6 %shard_map.112 = (bf16[512,512]{1,0:T(8,128)(2,1)S(1)}, bf16[512,512]{1,0:T(8,128)(2,1)S(1)}, f32[1,512]{1,0:T(1,128)S(1)}, bf16[512,512]{1,0:T(8,128)(2,1)S(1)}) custom-call(bf16[8,1024,512]{2,1,0:T(8,128)(2,1)S(1)} %shard_map.111.a_hbm, bf16[512,512]{1,0:T(8,128)(2,1)S(1)} %copy-done.1, bf16[512,512]{1,0:T(8,128)(2,1)S(1)} %copy-done.2, ...), custom_call_target="tpu_custom_call" | custom-call | tf_op jit(solution)/shard_map/pallas_call | solution.py:512
  130.7 1.1 convert_element_type.3
  131.8 0.8 copy.16
  132.6 0.6 copy.17
  133.1 0.8 copy.18
Async XLA Ops:
  0.6 7.4 %copy-start.4 = (f32[512]{0:T(512)S(1)}, f32[512]{0:T(512)}, u32[]{:S(2)}) copy-start(f32[512]{0:T(512)} %param.10) | copy-start | bytes 6148
  1.3 2.2 %copy-start = (bf16[1,1,128,128,128]{4,3,2,1,0:T(8,128)(2,1)S(1)}, bf16[1,1,128,128,128]{4,3,2,1,0:T(8,128)(2,1)}, u32[]{:S(2)}) copy-start(bf16[1,1,128,128,128]{4,3,2,1,0:T(8,128)(2,1)} %param.11) | copy-start | bytes 12582916
  3.5 0.7 copy-start.5
  4.1 0.7 copy-start.6
  4.8 3.2 %copy-start.1 = (bf16[512,512]{1,0:T(8,128)(2,1)S(1)}, bf16[512,512]{1,0:T(8,128)(2,1)}, u32[]{:S(2)}) copy-start(bf16[512,512]{1,0:T(8,128)(2,1)} %x_ref.1) | copy-start | bytes 1572868
  4.8 3.2 %copy-start.2 = (bf16[512,512]{1,0:T(8,128)(2,1)S(1)}, bf16[512,512]{1,0:T(8,128)(2,1)}, u32[]{:S(2)}) copy-start(bf16[512,512]{1,0:T(8,128)(2,1)} %w_ref.1) | copy-start | bytes 1572868
  4.8 3.2 %copy-start.3 = (bf16[512,512]{1,0:T(8,128)(2,1)S(1)}, bf16[512,512]{1,0:T(8,128)(2,1)}, u32[]{:S(2)}) copy-start(bf16[512,512]{1,0:T(8,128)(2,1)} %cot_ref.1) | copy-start | bytes 1572868

commit v3 on v2

--- a/solution.py
+++ b/solution.py
@@ -188,10 +188,10 @@
     a_hbm, x_ref, w_ref, b_ref, cot_ref,
     act_ref, wg_ref, bg_ref, fg_ref,
     av, xg, acc, psend, precv, gath, dpre_s, dg,
-    own, sbuf, srecv, csend, crecv, cmid,
+    own, sbuf, srecv, csend, crecv,
     fsum, wl, wra, wa, wab, wrb, wb, wrc, wfin, bs, br, br2,
     a_sem, gz_s, gz_r, gs_s, gs_r, p_s, p_r, d_s, d_r,
-    s_s, s_r, c_s, c_r, m_r, w_s, w_r, wz_s, wz_r, wf_s, wf_r, bz_s, bz_r, bx_s, bx_r,
+    s_s, s_r, c_s, c_r, w_s, w_r, wz_s, wz_r, wf_s, wf_r, bz_s, bz_r, bx_s, bx_r,
 ):
     r = lax.axis_index("row")
     c = lax.axis_index("col")
@@ -230,27 +230,23 @@
     def mirrored(position):
         return jnp.where(z * 2 < Z, position, Z - 1 - position)
 
-    def z_copy(h, t, dst, kind):
+    def z_copy(h, t, step):
         slot = xg.at[h, t, k]
-        return rc(slot, slot, gz_s.at[h, kind, dst], gz_r.at[h, t], at_z(dst))
+        return rc(slot, slot, gz_s.at[h, (1 - step) // 2, t], gz_r.at[h, t], at_z(z + step))
 
     def s_copy(h, t):
         slot = xg.at[h, t, k]
         return rc(slot, slot, gs_s.at[h, t], gs_r.at[h, t], sib)
 
-    def own_targets(h, act):
-        @pl.when(end)
+    def own_sends(h):
+        @pl.when(z < Z - 1)
         def _():
-            for position in (3, 2, 1):
-                act(z_copy(h, z, mirrored(position), 0))
-
-        @pl.when(jnp.logical_not(end))
+            z_copy(h, z, 1).start()
+
+        @pl.when(z > 0)
         def _():
-            for position in (2, 0):
-                act(z_copy(h, z, mirrored(position), 0))
-
-    def own_sends(h):
-        own_targets(h, lambda copy: copy.start())
+            z_copy(h, z, -1).start()
+
         s_copy(h, z).start()
 
     def mm(h, t, plane, first=False):
@@ -266,29 +262,42 @@
     def p_copy(h):
         return rc(psend.at[h], precv.at[h], p_s.at[h], p_r.at[h], peer)
 
-    own_sends(0)
+    def share(h):
+        psend[h] = acc[h, pl.ds(pl.multiple_of((1 - c) * V, V), V), :].astype(bf16)
+        p_copy(h).start()
+
+    for h in range(FC):
+        own_sends(h)
     for h in range(FC):
         mm(h, z, k, True)
+    for h in range(FC):
         got(xg.at[h, z, 1 - k], gs_r.at[h, z])
         mm(h, z, 1 - k)
-        for turn in range(Z - 1):
-            t = mirrored(jnp.where(end, (1, 3, 2)[turn], (2, 0, 3)[turn]))
-            got(xg.at[h, t, k], gz_r.at[h, t])
-            if turn == 0:
-
-                @pl.when(jnp.logical_not(end))
-                def _(t=t):
-                    z_copy(h, t, mirrored(0), 1).start()
-
-            s_copy(h, t).start()
-            if turn == 0 and h + 1 < FC:
-                own_sends(h + 1)
-            mm(h, t, k)
-            got(xg.at[h, t, 1 - k], gs_r.at[h, t])
-            mm(h, t, 1 - k)
-
-        psend[h] = acc[h, pl.ds(pl.multiple_of((1 - c) * V, V), V), :].astype(bf16)
-        p_copy(h).start()
+    for dist in range(1, Z):
+        for h in range(FC):
+            sides = ((z - dist, z - dist >= 0, 1), (z + dist, z + dist < Z, -1))
+            for t, valid, step in sides:
+
+                @pl.when(valid)
+                def _(h=h, t=t, step=step):
+                    got(xg.at[h, t, k], gz_r.at[h, t])
+
+                    @pl.when((z + step >= 0) & (z + step < Z))
+                    def _():
+                        z_copy(h, t, step).start()
+
+                    s_copy(h, t).start()
+
+            for t, valid, step in sides:
+
+                @pl.when(valid)
+                def _(h=h, t=t):
+                    mm(h, t, k)
+                    got(xg.at[h, t, 1 - k], gs_r.at[h, t])
+                    mm(h, t, 1 - k)
+
+            if dist == Z - 1:
+                share(h)
 
     pre = jnp.broadcast_to(b_ref[...], (V, F))
     for h in range(FC):
@@ -386,12 +395,10 @@
     def s2_copy(h, d):
         return rc(sbuf.at[h, d], srecv.at[h, d], s_s.at[h, d], s_r.at[h, d], sib)
 
-    def c_copy(h, d):
-        return rc(csend.at[h, d], crecv.at[h, z], c_s.at[h, d], c_r.at[h, z], at_z(d))
-
-    def mid_copy(h):
+    def c_copy(h, d, step):
+        place = jnp.where((step < 0) & (d == z - 1), Z, d)
         return rc(
-            csend.at[h, Z - 1 - z], cmid.at[h], c_s.at[h, Z - 1 - z], m_r.at[h], at_z(mirrored(1))
+            csend.at[h, d], crecv.at[h, place], c_s.at[h, d], c_r.at[h, place], at_z(z + step)
         )
 
     def bmm(h, d, plane):
@@ -407,21 +414,6 @@
         s2_copy(h, d).wait_recv()
         return own[h, d].astype(f32) + srecv[h, d].astype(f32)
 
-    def ship(h, i):
-        d = target(i)
-
-        @pl.when(end | (i != 1))
-        def _():
-            csend[h, d] = local_sum(h, d).astype(bf16)
-
-        @pl.when(end & (i == 0))
-        def _():
-            mid_copy(h).start()
-
-        @pl.when((end & (i != 0)) | (jnp.logical_not(end) & (i != 1)))
-        def _():
-            c_copy(h, d).start()
-
     def products(i, carry):
         d = target(i)
         for h in range(FC):
@@ -434,41 +426,48 @@
             s2_copy(h, d).start()
             own[h, d] = bmm(h, d, k)
 
-            @pl.when(i > 0)
+            @pl.when(end & (i < Z - 1))
             def _(h=h):
-                ship(h, i - 1)
+                csend[h, d] = local_sum(h, d).astype(bf16)
+                c_copy(h, d, jnp.where(z == 0, 1, -1)).start()
 
         return carry
 
-    def middle(h):
+    inward = jnp.where(z * 2 < Z, 1, -1)
+
+    def forward(d, step):
         @pl.when(jnp.logical_not(end))
         def _():
-            d = target(1)
-            got(cmid.at[h], m_r.at[h])
-            csend[h, d] = (local_sum(h, d) + cmid[h].astype(f32)).astype(bf16)
-            c_copy(h, d).start()
+            for h in range(FC):
+                got(crecv.at[h, d], c_r.at[h, d])
+                csend[h, d] = (local_sum(h, d) + crecv[h, d].astype(f32)).astype(bf16)
+                c_copy(h, d, step).start()
 
     def finish(h):
         s2_copy(h, z).wait_recv()
         fsum[...] = own[h, z].astype(f32) + srecv[h, z].astype(f32)
 
-        for src in range(Z):
-
-            @pl.when((z != src) & jnp.logical_not(end & (z == Z - 1 - src)))
-            def _(src=src):
-                got(crecv.at[h, src], c_r.at[h, src])
-                fsum[...] += crecv[h, src].astype(f32)
+        @pl.when(z > 0)
+        def _():
+            got(crecv.at[h, z], c_r.at[h, z])
+            fsum[...] += crecv[h, z].astype(f32)
+
+        @pl.when(z < Z - 1)
+        def _():
+            got(crecv.at[h, Z], c_r.at[h, Z])
+            fsum[...] += crecv[h, Z].astype(f32)
 
         fg_ref[:, h * fc : (h + 1) * fc] = fsum[...].T.astype(bf16)
 
     lax.fori_loop(0, Z, products, 0)
     stage_b()
-    for h in range(FC):
-        middle(h)
+    forward(mirrored(3), inward)
     stage_c()
+    forward(mirrored(0), -inward)
+    forward(mirrored(2), inward)
+    stage_d()
     for h in range(FC - 1):
         finish(h)
-    stage_d()
     stage_e()
     finish(FC - 1)
     stage_f()
@@ -476,19 +475,22 @@
     wg_ref[...] = wfin[...].reshape(F, F)
 
     for h in range(FC):
-        own_targets(h, lambda copy: copy.wait_send())
-
-        @pl.when(jnp.logical_not(end))
-        def _(h=h):
-            z_copy(h, mirrored(2), mirrored(0), 1).wait_send()
-
         for t in range(Z):
+
+            @pl.when((z < Z - 1) & (t <= z))
+            def _(h=h, t=t):
+                z_copy(h, t, 1).wait_send()
+
+            @pl.when((z > 0) & (t >= z))
+            def _(h=h, t=t):
+                z_copy(h, t, -1).wait_send()
+
             s_copy(h, t).wait_send()
             s2_copy(h, t).wait_send()
 
             @pl.when(z != t)
             def _(h=h, t=t):
-                c_copy(h, t).wait_send()
+                c_copy(h, t, jnp.where(z < t, 1, -1)).wait_send()
 
         p_copy(h).wait_send()
         d_copy(h).wait_send()
@@ -524,13 +526,13 @@
             vm((FC, V, fc), bf16), vm((FC, V, fc), bf16), vm((V, F), bf16), vm((V, F), bf16),
             vm((FC, 2, fc, V), bf16),
             vm((FC, Z, fc, V), bf16), vm((FC, Z, fc, V), bf16), vm((FC, Z, fc, V), bf16),
-            vm((FC, Z, fc, V), bf16), vm((FC, Z, fc, V), bf16), vm((FC, fc, V), bf16),
+            vm((FC, Z, fc, V), bf16), vm((FC, Z + 1, fc, V), bf16),
             vm((fc, V), f32), vm((F, F), f32), vm((H, F), f32), vm((H, F), f32), vm((Q, F), bf16), vm((Q, F), bf16),
             vm((Z, P8, F), bf16), vm((Z, P8, F), bf16), vm((2, 2, Z, P8, F), bf16),
             vm((3, 8, F), f32), vm((2, 8, F), f32), vm((Z, 8, F), f32),
             dma((R,)), dma((FC, 2, Z)), dma((FC, Z)), dma((FC, Z)), dma((FC, Z)),
             dma((FC,)), dma((FC,)), dma((FC,)), dma((FC,)),
-            dma((FC, Z)), dma((FC, Z)), dma((FC, Z)), dma((FC, Z)), dma((FC,)),
+            dma((FC, Z)), dma((FC, Z)), dma((FC, Z)), dma((FC, Z + 1)),
             dma((4,)), dma((4,)), dma((Z,)), dma((Z,)), dma((Z,)), dma((Z,)),
             dma((Z,)), dma((Z,)), dma((2,)), dma((2,)),
         ],

time: 135 us -> 124 us (0.919)
  Pallas kernels: 126 us -> 115 us
    pallas_call x1, Pallas kernels: 123 us -> 110 us  [fused_layer(): pl.pallas_call(functools.partial(layer_kernel, Z, FC, scale), out_shape=(...]
where the time goes in v3:
time: 124 us; the launch traced here: 123 us
  Pallas kernels  115 us (93%)
  local copies, waits for them, and re-layouts  5.67 us (5%)
  between operations  1.36 us (1%)
    pallas_call x1, Pallas kernels, fused_layer(): pl.pallas_call(functools.partial(layer_kernel, Z, FC, scale), out_shape=(...  110 us
    unnamed x17, local copies, waits for them, and re-layouts  5.67 us
    pallas_call x1, Pallas kernels, densify(): pl.pallas_call(body, out_shape=jax.ShapeDtypeStruct((steps, row_tiles * e...  4.42 us

profile of v3, /device:TPU:4, one launch (start us, length us, event | category | flops | bytes accessed | tf_op | source)
XLA Modules:
  0.0 122.8 jit_solution(14805388249788933604)
XLA Ops:
  0.6 0.0 copy-start.4
  1.3 0.0 copy-start
  1.3 2.2 %copy-done = bf16[1,1,128,128,128]{4,3,2,1,0:T(8,128)(2,1)S(1)} copy-done((bf16[1,1,128,128,128]{4,3,2,1,0:T(8,128)(2,1)S(1)}, bf16[1,1,128,128,128]{4,3,2,1,0:T(8,128)(2,1)}, u32[]{:S(2)}) %copy-start) | copy-done | bytes 4194328
  3.5 0.0 copy-start.5
  3.5 0.7 copy-done.5
  4.1 0.0 copy-start.6
  4.1 0.7 copy-done.6
  4.8 0.0 copy-start.1
  4.8 0.0 copy-start.2
  4.8 0.0 copy-start.3
  4.8 4.4 %shard_map.111.a_hbm = bf16[8,1024,512]{2,1,0:T(8,128)(2,1)S(1)} custom-call(s32[128]{0:T(128)S(1)} %bitcast.10, s32[128]{0:T(128)S(1)} %bitcast.11, s32[1]{0:T(128)} %bitcast.6.count_ref, bf16[128,128,128]{2,1,0:T(8,128)(2,1)S(1)} %bitcast.7), custom_call_target="tpu_custom_call" | custom-call | tf_op jit(solution)/shard_map/pallas_call | solution.py:167
  9.2 0.0 copy-done.4
  9.2 0.0 copy-done.1
  9.3 0.0 copy-done.2
  9.3 0.0 copy-done.3
  9.3 110.3 %shard_map.112 = (bf16[512,512]{1,0:T(8,128)(2,1)S(1)}, bf16[512,512]{1,0:T(8,128)(2,1)S(1)}, f32[1,512]{1,0:T(1,128)S(1)}, bf16[512,512]{1,0:T(8,128)(2,1)S(1)}) custom-call(bf16[8,1024,512]{2,1,0:T(8,128)(2,1)S(1)} %shard_map.111.a_hbm, bf16[512,512]{1,0:T(8,128)(2,1)S(1)} %copy-done.1, bf16[512,512]{1,0:T(8,128)(2,1)S(1)} %copy-done.2, ...), custom_call_target="tpu_custom_call" | custom-call | tf_op jit(solution)/shard_map/pallas_call | solution.py:514
  119.6 1.1 convert_element_type.3
  120.7 0.8 copy.16
  121.5 0.6 copy.17
  122.0 0.8 copy.18
Async XLA Ops:
  0.6 8.6 %copy-start.4 = (f32[512]{0:T(512)S(1)}, f32[512]{0:T(512)}, u32[]{:S(2)}) copy-start(f32[512]{0:T(512)} %param.10) | copy-start | bytes 6148
  1.3 2.2 %copy-start = (bf16[1,1,128,128,128]{4,3,2,1,0:T(8,128)(2,1)S(1)}, bf16[1,1,128,128,128]{4,3,2,1,0:T(8,128)(2,1)}, u32[]{:S(2)}) copy-start(bf16[1,1,128,128,128]{4,3,2,1,0:T(8,128)(2,1)} %param.11) | copy-start | bytes 12582916
  3.5 0.7 copy-start.5
  4.1 0.7 copy-start.6
  4.8 4.4 %copy-start.1 = (bf16[512,512]{1,0:T(8,128)(2,1)S(1)}, bf16[512,512]{1,0:T(8,128)(2,1)}, u32[]{:S(2)}) copy-start(bf16[512,512]{1,0:T(8,128)(2,1)} %x_ref.1) | copy-start | bytes 1572868
  4.8 4.5 %copy-start.2 = (bf16[512,512]{1,0:T(8,128)(2,1)S(1)}, bf16[512,512]{1,0:T(8,128)(2,1)}, u32[]{:S(2)}) copy-start(bf16[512,512]{1,0:T(8,128)(2,1)} %w_ref.1) | copy-start | bytes 1572868
  4.8 4.5 %copy-start.3 = (bf16[512,512]{1,0:T(8,128)(2,1)S(1)}, bf16[512,512]{1,0:T(8,128)(2,1)}, u32[]{:S(2)}) copy-start(bf16[512,512]{1,0:T(8,128)(2,1)} %cot_ref.1) | copy-start | bytes 1572868
